TPU v7x, 32 devices: a whole 2x2x4 slice. The times are simulated.
32 devices in a mesh: seq: 8 (over y, x, core), ch: 4 (over z).
Axes of the slice: x: 2, y: 2, z: 4, core: 2. Of those that a mesh axis runs over, the one named last changes fastest.
Arguments:
- inputs: bfloat16 [1536, 131072], P('ch', 'seq'), may hold values from -6 to 6
- gating: bfloat16 [1536, 131072], P('ch', 'seq'), may hold values from -6 to 6
- upstream: bfloat16 [1536, 131072], P('ch', 'seq'), may hold values from -6 to 6
- factor_one: bfloat16 [512, 512], replicated, may hold values from -0.25 to 0.25
- factor_two: bfloat16 [256, 256], replicated, may hold values from -0.375 to 0.375
- factor_three: bfloat16 [256, 256], replicated, may hold values from -0.375 to 0.375
- factor_four: bfloat16 [512, 512], replicated, may hold values from -0.25 to 0.25
- kernel_cols: float32 [1536, 512], P('ch'), may hold values from -4 to 4
- kernel_rows: float32 [1536, 256], P('ch'), may hold values from -4 to 4
Outputs:
- input_grad: bfloat16 [1536, 131072], P('ch', 'seq')
- gating_grad: bfloat16 [1536, 131072], P('ch', 'seq')
- one_grad: float32 [512, 512], replicated
- two_grad: float32 [256, 256], replicated
- three_grad: float32 [256, 256], replicated
- four_grad: float32 [512, 512], replicated
- cols_grad: float32 [1536, 512], P('ch')
- rows_grad: float32 [1536, 256], P('ch')
All inputs are finite; a program needn't handle non-finite values.
Results may differ from a plain program's by a relative error of at most 0.0076.
Values may be sent and summed in bfloat16 or wider, within the bound.
A program may use at most 384 MiB of HBM per device.

v0:
```python
import math
import jax
import jax.numpy as jnp
from jax import lax
from jax.sharding import PartitionSpec as P

P1 = 256
P2 = 512
C = 1536


def local(
    inputs,
    gating,
    upstream,
    factor_one,
    factor_two,
    factor_three,
    factor_four,
    kernel_cols,
    kernel_rows,
):
    width = inputs.shape[0]
    length = inputs.shape[1]
    parts = lax.axis_size("seq")
    flt = jnp.float32
    half = jnp.bfloat16
    rows_local = length // P2
    up_gate = (upstream.astype(flt) * gating.astype(flt)).astype(half)
    moved_in, moved_gate = (
        lax.all_to_all(inputs, "seq", split_axis=0, concat_axis=1, tiled=True),
        lax.all_to_all(up_gate, "seq", split_axis=0, concat_axis=1, tiled=True),
    )
    several = width // parts
    offset = lax.axis_index("seq") * several
    local_cols = lax.dynamic_slice_in_dim(kernel_cols, offset, several, 0)
    local_rows = lax.dynamic_slice_in_dim(kernel_rows, offset, several, 0)
    shaped = moved_in.reshape(several, P1, P2)
    gate_rows = moved_gate.reshape(several, P1, P2)
    first_prod = jnp.einsum("cij,jk->cik", shaped, factor_one, preferred_element_type=flt)
    first_out = (first_prod * local_cols[:, None, :]).astype(half)
    left_prod = jnp.einsum("ki,cij->ckj", factor_two, first_out, preferred_element_type=flt)
    left_out = (left_prod * local_rows[:, :, None]).astype(half)
    second = jnp.einsum("ki,cij->ckj", factor_three, left_out, preferred_element_type=flt).astype(
        half
    )
    grad_four = jnp.einsum("cij,cik->jk", second, gate_rows, preferred_element_type=flt)
    grad_second = jnp.einsum(
        "cik,jk->cij", gate_rows, factor_four, preferred_element_type=flt
    ).astype(half)
    grad_three = jnp.einsum("ckj,cij->ki", grad_second, left_out, preferred_element_type=flt)
    grad_left = jnp.einsum("ki,ckj->cij", factor_three, grad_second, preferred_element_type=flt)
    rows_part = jnp.sum(grad_left * left_prod, axis=2)
    grad_prod = (grad_left * local_rows[:, :, None]).astype(half)
    grad_two = jnp.einsum("ckj,cij->ki", grad_prod, first_out, preferred_element_type=flt)
    grad_first = jnp.einsum(
        "ki,ckj->cij", factor_two, grad_prod, preferred_element_type=flt
    ).astype(half)
    cols_part = jnp.sum(grad_first.astype(flt) * first_prod, axis=1)
    grad_inner = (grad_first.astype(flt) * local_cols[:, None, :]).astype(half)
    grad_one = jnp.einsum("cij,cik->jk", shaped, grad_inner, preferred_element_type=flt)
    local_input = jnp.einsum(
        "cik,jk->cij", grad_inner, factor_one, preferred_element_type=flt
    ).astype(half)
    input_grad, second_rows = (
        lax.all_to_all(
            local_input.reshape(several, P1 * P2), "seq", split_axis=1, concat_axis=0, tiled=True
        ),
        lax.all_to_all(
            second.reshape(several, P1 * P2), "seq", split_axis=1, concat_axis=0, tiled=True
        ),
    )
    cols_sum, rows_sum = (
        lax.all_gather(cols_part, "seq", axis=0, tiled=True),
        lax.all_gather(rows_part, "seq", axis=0, tiled=True),
    )
    final_prod = jnp.einsum(
        "cij,jk->cik",
        second_rows.reshape(width, rows_local, P2),
        factor_four,
        preferred_element_type=flt,
    )
    gating_grad = (
        (upstream.reshape(width, rows_local, P2).astype(flt) * final_prod)
        .astype(half)
        .reshape(width, length)
    )
    one_sum, two_sum, three_sum, four_sum = lax.psum(
        (grad_one, grad_two, grad_three, grad_four), ("seq", "ch")
    )
    scale_one = 1.0 / math.sqrt(P1 * C)
    scale_two = 1.0 / math.sqrt(P2 * C)
    return (
        input_grad,
        gating_grad,
        one_sum * scale_one,
        two_sum * scale_two,
        three_sum * scale_two,
        four_sum * scale_one,
        cols_sum / math.sqrt(P1),
        rows_sum / math.sqrt(P2),
    )


def solution(mesh):
    in_specs = (
        P("ch", "seq"),
        P("ch", "seq"),
        P("ch", "seq"),
        P(),
        P(),
        P(),
        P(),
        P("ch", None),
        P("ch", None),
    )
    out_specs = (P("ch", "seq"), P("ch", "seq"), P(), P(), P(), P(), P("ch", None), P("ch", None))
    return jax.shard_map(local, mesh=mesh, in_specs=in_specs, out_specs=out_specs, check_vma=False)
```

profile of v0, /device:TPU:0, one launch (start us, length us, event | category | flops | bytes accessed | tf_op | source)
XLA Modules:
  0.0 879.9 jit_solution(3477879930901490185)
XLA Ops:
  17.1 144.0 %all_to_all.67 = bf16[8,48,16384]{2,1,0:T(8,128)(2,1)} all-to-all(bf16[8,48,16384]{2,1,0:T(8,128)(2,1)S(1)} %bitcast.84), channel_id=1, replica_groups=mesh['seq'=8,'ch'=4] {'seq'}, dimensions={0} | all-to-all | bytes 25165824 | tf_op jit(solution)/shard_map/all_to_all | solution.py:32
  167.3 14.4 %copy.71 = bf16[48,8,16384]{2,1,0:T(8,128)(2,1)} copy(bf16[48,8,16384]{2,0,1:T(8,128)(2,1)} %bitcast.82) | data formatting | bytes 25165824 | tf_op jit(solution)/shard_map/all_to_all | solution.py:32
  181.7 19.5 %reshape.52 = bf16[48,256,512]{2,1,0:T(8,128)(2,1)} reshape(bf16[48,8,16384]{2,1,0:T(8,128)(2,1)} %copy.71) | data formatting | bytes 25165824 | tf_op jit(solution)/shard_map/reshape | solution.py:39
  227.5 14.8 %convolution_convert_fusion = bf16[48,512,256]{1,2,0:T(8,128)(2,1)} fusion(f32[48,512,256]{2,1,0:T(8,128)} %fusion.39, f32[48,256]{1,0:T(8,128)S(1)} %constant_dynamic-slice_fusion.1, bf16[256,256]{1,0:T(8,128)(2,1)S(1)} %copy-done.6), kind=kOutput, calls=%fused_computation.17 | convolution fusion | flops 3240099840 | bytes 37928960 | tf_op jit(solution)/shard_map/ki,ckj->cij/dot_general | solution.py:56
  256.7 19.8 %all_to_all.53 = bf16[48,8,16384]{2,1,0:T(8,128)(2,1)} reshape(bf16[48,256,512]{2,1,0:T(8,128)(2,1)} %fusion.10) | data formatting | bytes 25165824 | tf_op jit(solution)/shard_map/all_to_all | solution.py:66
  276.5 14.5 %copy.75 = bf16[48,8,16384]{2,0,1:T(8,128)(2,1)} copy(bf16[48,8,16384]{2,1,0:T(8,128)(2,1)} %all_to_all.53) | data formatting | bytes 25165824 | tf_op jit(solution)/shard_map/all_to_all | solution.py:66
  291.0 14.5 %all-to-all-done.2 = bf16[8,48,16384]{2,1,0:T(8,128)(2,1)} async-done(((bf16[8,48,16384]{2,1,0:T(8,128)(2,1)}), bf16[8,48,16384]{2,1,0:T(8,128)(2,1)}, u32[]{:S(2)}, u32[]{:S(2)}) %all-to-all-start.2) | async-done | bytes 12582944 | tf_op jit(solution)/shard_map/all_to_all | solution.py:31
  310.8 17.6 %copy.76 = f32[384,16384]{0,1:T(8,128)} copy(bf16[384,16384]{1,0:T(8,128)(2,1)} %param.11) | data formatting | bytes 37748736 | tf_op jit(solution)/shard_map/convert_element_type | solution.py:29
  328.4 24.6 %copy.82 = f32[384,32,512]{2,0,1:T(8,128)} copy(f32[384,32,512]{0,2,1:T(8,128)} %bitcast.80) | data formatting | bytes 50331648 | tf_op jit(solution)/shard_map/convert_element_type | solution.py:84
  367.4 19.5 %reshape.53 = bf16[48,256,512]{2,1,0:T(8,128)(2,1)} reshape(bf16[48,8,16384]{2,1,0:T(8,128)(2,1)} %copy.77) | data formatting | bytes 25165824 | tf_op jit(solution)/shard_map/reshape | solution.py:38
  387.0 18.9 %fusion.1 = (f32[48,512]{1,0:T(8,128)}, f32[48,256,512]{2,1,0:T(8,128)}) fusion(bf16[48,512,256]{1,2,0:T(8,128)(2,1)} %convolution_convert_fusion, bf16[48,256,512]{2,1,0:T(8,128)(2,1)} %reshape.53, bf16[512,512]{1,0:T(8,128)(2,1)S(1)} %copy-done.3), kind=kOutput, calls=%fused_computation.3 | convolution fusion | flops 6461300736 | bytes 50954240 | tf_op jit(solution)/shard_map/cij,jk->cik/dot_general | solution.py:40
  405.9 16.3 %fusion.21 = f32[48,512,256]{2,1,0:T(8,128)} fusion(f32[48,256,512]{2,1,0:T(8,128)} %get-tuple-element.45, f32[48,512]{1,0:T(8,128)S(1)} %constant_dynamic-slice_fusion, bf16[256,256]{1,0:T(8,128)(2,1)S(1)} %copy-done.6), kind=kOutput, calls=%fused_computation.22 | convolution fusion | flops 3233808384 | bytes 50561024 | tf_op jit(solution)/shard_map/ki,cij->ckj/dot_general | solution.py:42
  422.2 14.5 %convert_bitcast_fusion = bf16[48,256,512]{1,2,0:T(8,128)(2,1)} fusion(f32[48,512,256]{2,1,0:T(8,128)} %fusion.21, f32[48,256]{1,0:T(8,128)S(1)} %constant_dynamic-slice_fusion.1, bf16[256,256]{1,0:T(8,128)(2,1)S(1)} %copy-done.7), kind=kOutput, calls=%fused_computation.14 | convolution fusion | flops 3240099840 | bytes 37928960 | tf_op jit(solution)/shard_map/ki,cij->ckj/dot_general | solution.py:44
  436.7 16.7 %copy.79 = bf16[48,256,512]{2,1,0:T(8,128)(2,1)} copy(bf16[48,256,512]{1,2,0:T(8,128)(2,1)} %convert_bitcast_fusion) | data formatting | bytes 25165824 | tf_op jit(solution)/shard_map/convert_element_type | solution.py:44
  453.4 19.5 %all_to_all.60 = bf16[48,8,16384]{2,1,0:T(8,128)(2,1)} reshape(bf16[48,256,512]{2,1,0:T(8,128)(2,1)} %copy.79) | data formatting | bytes 25165824 | tf_op jit(solution)/shard_map/all_to_all | solution.py:69
  472.9 26.0 %copy.80 = bf16[48,8,16384]{2,0,1:T(8,128)(2,1)} copy(bf16[48,8,16384]{2,1,0:T(8,128)(2,1)} %all_to_all.60) | data formatting | bytes 25165824 | tf_op jit(solution)/shard_map/all_to_all | solution.py:69
  499.0 16.0 %fusion.28 = f32[256,256]{1,0:T(8,128)} fusion(bf16[48,256,512]{2,1,0:T(8,128)(2,1)} %copy-done.2, f32[48,512,256]{2,1,0:T(8,128)} %fusion.21, f32[48,256]{1,0:T(8,128)S(1)} %constant_dynamic-slice_fusion.1), kind=kOutput, calls=%fused_computation.26 | convolution fusion | flops 3233808384 | bytes 38060032 | tf_op jit(solution)/shard_map/ckj,cij->ki/dot_general | solution.py:51
  547.0 17.6 %fusion.25 = f32[256,256]{1,0:T(8,128)} fusion(f32[48,256,512]{2,1,0:T(8,128)} %get-tuple-element.45, f32[48,512]{1,0:T(8,128)S(1)} %constant_dynamic-slice_fusion, f32[48,512,256]{2,1,0:T(8,128)} %fusion.39, f32[48,256]{1,0:T(8,128)S(1)} %constant_dynamic-slice_fusion.1), kind=kOutput, calls=%fused_computation.25 | convolution fusion | flops 3246391296 | bytes 50741248 | tf_op jit(solution)/shard_map/ckj,cij->ki/dot_general | solution.py:55
  564.6 16.7 %multiply_reduce_fusion = f32[48,256]{1,0:T(8,128)S(1)} fusion(f32[48,512,256]{2,1,0:T(8,128)} %fusion.39, f32[48,512,256]{2,1,0:T(8,128)} %fusion.21), kind=kLoop, calls=%fused_computation.4 | loop fusion | flops 12570624 | bytes 50380800 | tf_op jit(solution)/shard_map/reduce_sum | solution.py:53
  581.3 89.7 %all_gather.7 = f32[384,256]{1,0:T(8,128)S(1)} all-gather(f32[48,256]{1,0:T(8,128)S(1)} %multiply_reduce_fusion), channel_id=1, replica_groups=mesh['seq'=8,'ch'=4] {'seq'}, dimensions={0}, use_global_device_ids=true | all-gather | bytes 442368 | tf_op jit(solution)/shard_map/all_gather | solution.py:75
  682.0 62.6 %all-reduce.3.cloned.1.call-done = (f32[512,512]{0,1:T(8,128)}, f32[256,256]{1,0:T(8,128)}, f32[256,256]{1,0:T(8,128)}, f32[512,512]{0,1:T(8,128)}) async-done(((f32[512,512]{0,1:T(8,128)}, f32[256,256]{1,0:T(8,128)}, f32[256,256]{1,0:T(8,128)}, f32[512,512]{0,1:T(8,128)}), (f32[512,512]{0,1:T(8,128)}, f32[256,256]{1,0:T(8,128)}, f32[256,256]{1,0:T(8,128)}, ...) | async-done | bytes 2621456 | tf_op jit(solution)/shard_map/psum | solution.py:88
  763.6 65.3 %multiply_convert_fusion = bf16[384,32,512]{2,0,1:T(8,128)(2,1)} fusion(f32[384,32,512]{2,0,1:T(8,128)} %copy.82, bf16[384,32,512]{2,1,0:T(8,128)(2,1)} %bitcast.81, bf16[512,512]{1,0:T(8,128)(2,1)S(1)} %copy-done.5), kind=kOutput, calls=%fused_computation.5 | convolution fusion | flops 6455033856 | bytes 50855936 | tf_op jit(solution)/shard_map/cij,jk->cik/dot_general | solution.py:77
  828.9 16.7 %copy.83 = bf16[384,32,512]{0,2,1:T(8,128)(2,1)} copy(bf16[384,32,512]{2,0,1:T(8,128)(2,1)} %multiply_convert_fusion) | data formatting | bytes 25165824 | tf_op jit(solution)/shard_map/convert_element_type | solution.py:85
  845.6 16.6 %copy.88 = bf16[384,16384]{1,0:T(8,128)(2,1)} copy(bf16[384,16384]{0,1:T(8,128)(2,1)} %bitcast.83) | data formatting | bytes 25165824
  (43 shorter events, 149.1 us)
Async XLA Ops:
  7.2 160.1 %copy-start = (f32[384,512]{1,0:T(8,128)S(1)}, f32[384,512]{1,0:T(8,128)}, u32[]{:S(2)}) copy-start(f32[384,512]{1,0:T(8,128)} %param.16) | copy-start | bytes 2359300
  161.1 144.4 %all-to-all-start.2 = ((bf16[8,48,16384]{2,1,0:T(8,128)(2,1)}), bf16[8,48,16384]{2,1,0:T(8,128)(2,1)}, u32[]{:S(2)}, u32[]{:S(2)}) async-start(bf16[8,48,16384]{2,1,0:T(8,128)(2,1)} %bitcast.85), calls=%async_computation.2 | async-start | bytes 25165824 | tf_op jit(solution)/shard_map/all_to_all | solution.py:31
  181.7 19.5 %copy-start.4 = (bf16[512,512]{1,0:T(8,128)(2,1)S(1)}, bf16[512,512]{1,0:T(8,128)(2,1)}, u32[]{:S(2)}) copy-start(bf16[512,512]{1,0:T(8,128)(2,1)} %param.15) | copy-start | bytes 1572868
  201.3 16.1 %copy-start.7 = (bf16[256,256]{1,0:T(8,128)(2,1)S(1)}, bf16[256,256]{1,0:T(8,128)(2,1)}, u32[]{:S(2)}) copy-start(bf16[256,256]{1,0:T(8,128)(2,1)} %param.14) | copy-start | bytes 393220
  212.8 4.5 copy-start.2
  217.4 10.1 %copy-start.6 = (bf16[256,256]{1,0:T(8,128)(2,1)S(1)}, bf16[256,256]{1,0:T(8,128)(2,1)}, u32[]{:S(2)}) copy-start(bf16[256,256]{1,0:T(8,128)(2,1)} %param.13) | copy-start | bytes 393220
  227.5 14.8 %copy-start.3 = (bf16[512,512]{1,0:T(8,128)(2,1)S(1)}, bf16[512,512]{1,0:T(8,128)(2,1)}, u32[]{:S(2)}) copy-start(bf16[512,512]{1,0:T(8,128)(2,1)} %param.12) | copy-start | bytes 1572868
  305.4 209.5 %all-to-all-start.1 = ((bf16[48,8,16384]{2,0,1:T(8,128)(2,1)}), bf16[48,8,16384]{2,0,1:T(8,128)(2,1)}, u32[]{:S(2)}, u32[]{:S(2)}) async-start(bf16[48,8,16384]{2,0,1:T(8,128)(2,1)} %copy.75), calls=%async_computation.1 | async-start | bytes 25165824 | tf_op jit(solution)/shard_map/all_to_all | solution.py:66
  514.9 235.9 %all-to-all-start.3 = ((bf16[48,8,16384]{2,0,1:T(8,128)(2,1)}), bf16[48,8,16384]{2,0,1:T(8,128)(2,1)}, u32[]{:S(2)}, u32[]{:S(2)}) async-start(bf16[48,8,16384]{2,0,1:T(8,128)(2,1)} %copy.80), calls=%async_computation.3 | async-start | bytes 25165824 | tf_op jit(solution)/shard_map/all_to_all | solution.py:69
  520.3 224.3 %all-reduce.3.cloned.1.call-start = ((), (), s32[]{:S(2)}) async-start(), calls=%async_computation.4 | async-start | bytes 5242880 | tf_op jit(solution)/shard_map/psum | solution.py:88
  564.6 106.4 %copy-start.8 = (f32[48,512]{1,0:T(8,128)S(1)}, f32[48,512]{1,0:T(8,128)}, u32[]{:S(2)}) copy-start(f32[48,512]{1,0:T(8,128)} %get-tuple-element.44) | copy-start | bytes 294916
  750.8 12.8 %copy-start.5 = (bf16[512,512]{1,0:T(8,128)(2,1)S(1)}, bf16[512,512]{1,0:T(8,128)(2,1)}, u32[]{:S(2)}) copy-start(bf16[512,512]{1,0:T(8,128)(2,1)} %param.15) | copy-start | bytes 1572868
  862.2 10.5 %copy-start.1 = (f32[384,512]{1,0:T(8,128)S(1)}, f32[384,512]{1,0:T(8,128)}, u32[]{:S(2)}) copy-start(f32[384,512]{1,0:T(8,128)} %param.16) | copy-start | bytes 2359300
Sparse Core Ops, SparseCore 0:
  564.7 179.7 all-reduce.2
where the time goes:
time: 894 us; the launch traced here: 880 us
  local copies, waits for them, and re-layouts  271 us (30%)
  blocking collectives  243 us (27%)
  matrix products  226 us (25%)
  waiting for transfers between devices  77.1 us (9%)
  other arithmetic  31.9 us (4%)
  starting transfers between devices  16.1 us (2%)
  between operations  14.5 us (2%)
    all_to_all x1, blocking collectives, local(): lax.all_to_all(up_gate, 'seq', split_axis=0, concat_axis=1, tiled=True)  144 us
    all_gather x1, blocking collectives, local(): lax.all_gather(rows_part, 'seq', axis=0, tiled=True)  89.7 us
    dot_general x1, matrix products, local(): jnp.einsum('cij,jk->cik', second_rows.reshape(width, rows_local, P2), fac...  65.3 us
    psum x1, waiting for transfers between devices, local(): lax.psum((grad_one, grad_two, grad_three, grad_four), ('seq', 'ch'))  62.6 us
    unnamed x23, local copies, waits for them, and re-layouts  47.1 us
    all_to_all x2, local copies, waits for them, and re-layouts, local(): lax.all_to_all(second.reshape(several, P1 * P2), 'seq', split_axis=1, con...  45.5 us
    all_to_all x2, local copies, waits for them, and re-layouts, local(): lax.all_to_all(local_input.reshape(several, P1 * P2), 'seq', split_axis=1...  34.3 us
    convert_element_type x1, local copies, waits for them, and re-layouts, local(): upstream.reshape(width, rows_local, P2).astype(flt) * final_prod  24.6 us
  transfers between devices with their start and end apart: 4, of which 2 were waited for; matrix products, arithmetic and copies ran while one was open for 40% of the time, Pallas kernels for 0%

commit v1 on v0

--- a/solution.py
+++ b/solution.py
@@ -7,6 +7,12 @@
 P1 = 256
 P2 = 512
 C = 1536
+
+
+def exchange_blocks(x, mesh_axis, split, join):
+    pieces = jnp.split(x, lax.axis_size(mesh_axis), axis=split)
+    received = lax.all_to_all(jnp.stack(pieces), mesh_axis, 0, 0)
+    return jnp.concatenate(received, axis=join)
 
 
 def local(
@@ -66,9 +72,7 @@
         lax.all_to_all(
             local_input.reshape(several, P1 * P2), "seq", split_axis=1, concat_axis=0, tiled=True
         ),
-        lax.all_to_all(
-            second.reshape(several, P1 * P2), "seq", split_axis=1, concat_axis=0, tiled=True
-        ),
+        exchange_blocks(second.reshape(several, P1 * P2), "seq", 1, 0),
     )
     cols_sum, rows_sum = (
         lax.all_gather(cols_part, "seq", axis=0, tiled=True),

time: 894 us -> 944 us (1.056)
  waiting for transfers between devices: 77.1 us -> 287 us
  blocking collectives: 243 us -> 98.8 us
  local copies, waits for them, and re-layouts: 271 us -> 247 us
    all_to_all x1 -> x0, blocking collectives: 144 us -> none  [local(): lax.all_to_all(up_gate, 'seq', split_axis=0, concat_axis=1, tiled=True)]
    all_to_all x1, waiting for transfers between devices: 14.5 us -> 126 us  [local(): lax.all_to_all(inputs, 'seq', split_axis=0, concat_axis=1, tiled=True)]
    all_to_all x1 -> x2, waiting for transfers between devices: 0.01 us -> 61.9 us  [the longest x1 61.9 us: local(): lax.all_to_all(up_gate, 'seq', split_axis=0, concat_axis=1, tiled=True)]
    all_to_all x2 -> x0, local copies, waits for them, and re-layouts: 45.5 us -> none  [local(): lax.all_to_all(second.reshape(several, P1 * P2), 'seq', split_axis=1, con...]
    all_to_all x1, waiting for transfers between devices: 0.01 us -> 35.7 us  [local(): lax.all_to_all(local_input.reshape(several, P1 * P2), 'seq', split_axis=1...]
    unnamed x23 -> x31, local copies, waits for them, and re-layouts: 47.1 us -> 82.2 us
    convert_element_type x1 -> x0, local copies, waits for them, and re-layouts: 16.7 us -> none  [local(): jnp.einsum('ki,cij->ckj', factor_three, left_out, preferred_element_type=...]
  transfers between devices with their start and end apart: 4 -> 5, of which waited for: 2 -> 4; matrix products, arithmetic and copies ran while one was open for 40% -> 28% of each run, Pallas kernels for 0% -> 0%
where the time goes in v1:
time: 944 us; the launch traced here: 930 us
  waiting for transfers between devices  287 us (30%)
  local copies, waits for them, and re-layouts  247 us (26%)
  matrix products  226 us (24%)
  blocking collectives  98.8 us (10%)
  other arithmetic  35.8 us (4%)
  starting transfers between devices  21.5 us (2%)
  between operations  14.5 us (2%)
    all_to_all x1, waiting for transfers between devices, local(): lax.all_to_all(inputs, 'seq', split_axis=0, concat_axis=1, tiled=True)  126 us
    all_gather x1, blocking collectives, local(): lax.all_gather(rows_part, 'seq', axis=0, tiled=True)  89.5 us
    unnamed x31, local copies, waits for them, and re-layouts  82.2 us
    dot_general x1, matrix products, local(): jnp.einsum('cij,jk->cik', second_rows.reshape(width, rows_local, P2), fac...  65.3 us
    psum x1, waiting for transfers between devices, local(): lax.psum((grad_one, grad_two, grad_three, grad_four), ('seq', 'ch'))  63.3 us
    all_to_all x1, waiting for transfers between devices, local(): lax.all_to_all(up_gate, 'seq', split_axis=0, concat_axis=1, tiled=True)  61.9 us
    all_to_all x1, waiting for transfers between devices, local(): lax.all_to_all(local_input.reshape(several, P1 * P2), 'seq', split_axis=1...  35.7 us
    all_to_all x2, local copies, waits for them, and re-layouts, local(): lax.all_to_all(local_input.reshape(several, P1 * P2), 'seq', split_axis=1...  34.1 us
  transfers between devices with their start and end apart: 5, of which 4 were waited for; matrix products, arithmetic and copies ran while one was open for 28% of the time, Pallas kernels for 0%

profile of v1, /device:TPU:0, one launch (start us, length us, event | category | flops | bytes accessed | tf_op | source)
XLA Modules:
  0.0 930.5 jit_solution(7112915644549785530)
XLA Ops:
  26.5 125.9 %all-to-all-done.2 = bf16[8,48,16384]{2,1,0:T(8,128)(2,1)} async-done(((bf16[8,48,16384]{2,1,0:T(8,128)(2,1)}), bf16[8,48,16384]{2,1,0:T(8,128)(2,1)}, u32[]{:S(2)}, u32[]{:S(2)}) %all-to-all-start.2) | async-done | bytes 12582944 | tf_op jit(solution)/shard_map/all_to_all | solution.py:37
  157.7 17.6 %copy.74 = f32[384,16384]{0,1:T(8,128)} copy(bf16[384,16384]{1,0:T(8,128)(2,1)} %param.11) | data formatting | bytes 37748736 | tf_op jit(solution)/shard_map/convert_element_type | solution.py:35
  175.3 24.7 %copy.79 = f32[384,32,512]{2,0,1:T(8,128)} copy(f32[384,32,512]{0,2,1:T(8,128)} %bitcast.115) | data formatting | bytes 50331648 | tf_op jit(solution)/shard_map/convert_element_type | solution.py:88
  200.8 14.4 %copy.75 = bf16[48,8,16384]{2,1,0:T(8,128)(2,1)} copy(bf16[48,8,16384]{2,0,1:T(8,128)(2,1)} %bitcast.12) | data formatting | bytes 25165824 | tf_op jit(solution)/shard_map/all_to_all | solution.py:37
  215.3 19.6 %reshape.47 = bf16[48,256,512]{2,1,0:T(8,128)(2,1)} reshape(bf16[48,8,16384]{2,1,0:T(8,128)(2,1)} %copy.75) | data formatting | bytes 25165824 | tf_op jit(solution)/shard_map/reshape | solution.py:44
  234.8 61.9 %all-to-all-done = bf16[8,48,16384]{2,1,0:T(8,128)(2,1)} async-done(((bf16[8,48,16384]{2,1,0:T(8,128)(2,1)}), bf16[8,48,16384]{2,1,0:T(8,128)(2,1)}, u32[]{:S(2)}, u32[]{:S(2)}) %all-to-all-start) | async-done | bytes 12582944 | tf_op jit(solution)/shard_map/all_to_all | solution.py:38
  296.7 14.4 %copy.69 = bf16[48,8,16384]{2,1,0:T(8,128)(2,1)} copy(bf16[48,8,16384]{2,0,1:T(8,128)(2,1)} %bitcast.1) | data formatting | bytes 25165824 | tf_op jit(solution)/shard_map/all_to_all | solution.py:38
  311.1 19.5 %reshape.46 = bf16[48,256,512]{2,1,0:T(8,128)(2,1)} reshape(bf16[48,8,16384]{2,1,0:T(8,128)(2,1)} %copy.69) | data formatting | bytes 25165824 | tf_op jit(solution)/shard_map/reshape | solution.py:45
  356.9 14.8 %convolution_convert_fusion = bf16[48,512,256]{1,2,0:T(8,128)(2,1)} fusion(f32[48,512,256]{2,1,0:T(8,128)} %fusion.47, f32[48,256]{1,0:T(8,128)S(1)} %constant_dynamic-slice_fusion.1, bf16[256,256]{1,0:T(8,128)(2,1)S(1)} %copy-done.6), kind=kOutput, calls=%fused_computation.17 | convolution fusion | flops 3240099840 | bytes 37928960 | tf_op jit(solution)/shard_map/ki,ckj->cij/dot_general | solution.py:62
  371.7 14.6 %fusion.10 = bf16[48,256,512]{2,1,0:T(8,128)(2,1)} fusion(bf16[48,512,256]{1,2,0:T(8,128)(2,1)} %convolution_convert_fusion, f32[48,512]{1,0:T(8,128)S(1)} %constant_dynamic-slice_fusion, bf16[512,512]{1,0:T(8,128)(2,1)S(1)} %copy-done.3), kind=kOutput, calls=%fused_computation.18 | convolution fusion | flops 6467616768 | bytes 25788416 | tf_op jit(solution)/shard_map/cik,jk->cij/dot_general | solution.py:68
  386.3 19.6 %all_to_all.44 = bf16[48,8,16384]{2,1,0:T(8,128)(2,1)} reshape(bf16[48,256,512]{2,1,0:T(8,128)(2,1)} %fusion.10) | data formatting | bytes 25165824 | tf_op jit(solution)/shard_map/all_to_all | solution.py:72
  405.9 14.5 %copy.73 = bf16[48,8,16384]{2,0,1:T(8,128)(2,1)} copy(bf16[48,8,16384]{2,1,0:T(8,128)(2,1)} %all_to_all.44) | data formatting | bytes 25165824 | tf_op jit(solution)/shard_map/all_to_all | solution.py:72
  425.7 18.9 %fusion.1 = (f32[48,512]{1,0:T(8,128)}, f32[48,256,512]{2,1,0:T(8,128)}) fusion(bf16[48,512,256]{1,2,0:T(8,128)(2,1)} %convolution_convert_fusion, bf16[48,256,512]{2,1,0:T(8,128)(2,1)} %reshape.47, bf16[512,512]{1,0:T(8,128)(2,1)S(1)} %copy-done.3), kind=kOutput, calls=%fused_computation.3 | convolution fusion | flops 6461300736 | bytes 50954240 | tf_op jit(solution)/shard_map/cij,jk->cik/dot_general | solution.py:46
  444.6 16.3 %fusion.21 = f32[48,512,256]{2,1,0:T(8,128)} fusion(f32[48,256,512]{2,1,0:T(8,128)} %get-tuple-element.45, f32[48,512]{1,0:T(8,128)S(1)} %constant_dynamic-slice_fusion, bf16[256,256]{1,0:T(8,128)(2,1)S(1)} %copy-done.6), kind=kOutput, calls=%fused_computation.22 | convolution fusion | flops 3233808384 | bytes 50561024 | tf_op jit(solution)/shard_map/ki,cij->ckj/dot_general | solution.py:48
  475.3 16.4 %copy.98 = bf16[6,8,256,512]{3,1,2,0:T(8,128)(2,1)} copy(bf16[6,8,256,512]{2,3,1,0:T(8,128)(2,1)} %bitcast.114) | data formatting | bytes 25165824
  505.1 15.8 %fusion.36 = f32[256,256]{1,0:T(8,128)} fusion(bf16[48,256,512]{2,1,0:T(8,128)(2,1)} %copy-done.2, f32[48,512,256]{2,1,0:T(8,128)} %fusion.21, f32[48,256]{1,0:T(8,128)S(1)} %constant_dynamic-slice_fusion.1), kind=kOutput, calls=%fused_computation.42 | convolution fusion | flops 3233808384 | bytes 38060032 | tf_op jit(solution)/shard_map/ckj,cij->ki/dot_general | solution.py:57
  529.0 35.7 %all-to-all-done.1 = bf16[48,8,16384]{2,0,1:T(8,128)(2,1)} async-done(((bf16[48,8,16384]{2,0,1:T(8,128)(2,1)}), bf16[48,8,16384]{2,0,1:T(8,128)(2,1)}, u32[]{:S(2)}, u32[]{:S(2)}) %all-to-all-start.1) | async-done | bytes 12582944 | tf_op jit(solution)/shard_map/all_to_all | solution.py:72
  597.0 17.6 %fusion.33 = f32[256,256]{1,0:T(8,128)} fusion(f32[48,256,512]{2,1,0:T(8,128)} %get-tuple-element.45, f32[48,512]{1,0:T(8,128)S(1)} %constant_dynamic-slice_fusion, f32[48,512,256]{2,1,0:T(8,128)} %fusion.47, f32[48,256]{1,0:T(8,128)S(1)} %constant_dynamic-slice_fusion.1), kind=kOutput, calls=%fused_computation.41 | convolution fusion | flops 3246391296 | bytes 50741248 | tf_op jit(solution)/shard_map/ckj,cij->ki/dot_general | solution.py:61
  614.6 16.6 %multiply_reduce_fusion = f32[48,256]{1,0:T(8,128)S(1)} fusion(f32[48,512,256]{2,1,0:T(8,128)} %fusion.47, f32[48,512,256]{2,1,0:T(8,128)} %fusion.21), kind=kLoop, calls=%fused_computation.4 | loop fusion | flops 12570624 | bytes 50380800 | tf_op jit(solution)/shard_map/reduce_sum | solution.py:59
  631.3 89.5 %all_gather.7 = f32[384,256]{1,0:T(8,128)S(1)} all-gather(f32[48,256]{1,0:T(8,128)S(1)} %multiply_reduce_fusion), channel_id=1, replica_groups=mesh['seq'=8,'ch'=4] {'seq'}, dimensions={0}, use_global_device_ids=true | all-gather | bytes 442368 | tf_op jit(solution)/shard_map/all_gather | solution.py:79
  731.8 63.3 %all-reduce.3.cloned.1.call-done = (f32[512,512]{0,1:T(8,128)}, f32[256,256]{1,0:T(8,128)}, f32[256,256]{1,0:T(8,128)}, f32[512,512]{0,1:T(8,128)}) async-done(((f32[512,512]{0,1:T(8,128)}, f32[256,256]{1,0:T(8,128)}, f32[256,256]{1,0:T(8,128)}, f32[512,512]{0,1:T(8,128)}), (f32[512,512]{0,1:T(8,128)}, f32[256,256]{1,0:T(8,128)}, f32[256,256]{1,0:T(8,128)}, ...) | async-done | bytes 2621456 | tf_op jit(solution)/shard_map/psum | solution.py:92
  814.2 65.3 %multiply_convert_fusion = bf16[384,32,512]{2,0,1:T(8,128)(2,1)} fusion(f32[384,32,512]{2,0,1:T(8,128)} %copy.79, bf16[384,32,512]{2,1,0:T(8,128)(2,1)} %bitcast.116, bf16[512,512]{1,0:T(8,128)(2,1)S(1)} %copy-done.5), kind=kOutput, calls=%fused_computation.5 | convolution fusion | flops 6455033856 | bytes 50855936 | tf_op jit(solution)/shard_map/cij,jk->cik/dot_general | solution.py:81
  879.5 16.6 %copy.80 = bf16[384,32,512]{0,2,1:T(8,128)(2,1)} copy(bf16[384,32,512]{2,0,1:T(8,128)(2,1)} %multiply_convert_fusion) | data formatting | bytes 25165824 | tf_op jit(solution)/shard_map/convert_element_type | solution.py:89
  896.1 16.6 %copy.85 = bf16[384,16384]{1,0:T(8,128)(2,1)} copy(bf16[384,16384]{0,1:T(8,128)(2,1)} %bitcast.125) | data formatting | bytes 25165824
  (50 shorter events, 165.7 us)
Async XLA Ops:
  7.2 193.7 %copy-start = (f32[384,512]{1,0:T(8,128)S(1)}, f32[384,512]{1,0:T(8,128)}, u32[]{:S(2)}) copy-start(f32[384,512]{1,0:T(8,128)} %param.16) | copy-start | bytes 2359300
  7.2 145.2 %all-to-all-start.2 = ((bf16[8,48,16384]{2,1,0:T(8,128)(2,1)}), bf16[8,48,16384]{2,1,0:T(8,128)(2,1)}, u32[]{:S(2)}, u32[]{:S(2)}) async-start(bf16[8,48,16384]{2,1,0:T(8,128)(2,1)} %bitcast.127), calls=%async_computation.2 | async-start | bytes 25165824 | tf_op jit(solution)/shard_map/all_to_all | solution.py:37
  152.4 144.3 %all-to-all-start = ((bf16[8,48,16384]{2,1,0:T(8,128)(2,1)}), bf16[8,48,16384]{2,1,0:T(8,128)(2,1)}, u32[]{:S(2)}, u32[]{:S(2)}) async-start(bf16[8,48,16384]{2,1,0:T(8,128)(2,1)} %bitcast.126), calls=%async_computation | async-start | bytes 25165824 | tf_op jit(solution)/shard_map/all_to_all | solution.py:38
  311.1 19.5 %copy-start.4 = (bf16[512,512]{1,0:T(8,128)(2,1)S(1)}, bf16[512,512]{1,0:T(8,128)(2,1)}, u32[]{:S(2)}) copy-start(bf16[512,512]{1,0:T(8,128)(2,1)} %param.15) | copy-start | bytes 1572868
  330.7 16.1 %copy-start.7 = (bf16[256,256]{1,0:T(8,128)(2,1)S(1)}, bf16[256,256]{1,0:T(8,128)(2,1)}, u32[]{:S(2)}) copy-start(bf16[256,256]{1,0:T(8,128)(2,1)} %param.14) | copy-start | bytes 393220
  342.3 4.5 copy-start.2
  346.8 10.1 %copy-start.6 = (bf16[256,256]{1,0:T(8,128)(2,1)S(1)}, bf16[256,256]{1,0:T(8,128)(2,1)}, u32[]{:S(2)}) copy-start(bf16[256,256]{1,0:T(8,128)(2,1)} %param.13) | copy-start | bytes 393220
  356.9 14.8 %copy-start.3 = (bf16[512,512]{1,0:T(8,128)(2,1)S(1)}, bf16[512,512]{1,0:T(8,128)(2,1)}, u32[]{:S(2)}) copy-start(bf16[512,512]{1,0:T(8,128)(2,1)} %param.12) | copy-start | bytes 1572868
  420.4 144.3 %all-to-all-start.1 = ((bf16[48,8,16384]{2,0,1:T(8,128)(2,1)}), bf16[48,8,16384]{2,0,1:T(8,128)(2,1)}, u32[]{:S(2)}, u32[]{:S(2)}) async-start(bf16[48,8,16384]{2,0,1:T(8,128)(2,1)} %copy.73), calls=%async_computation.1 | async-start | bytes 25165824 | tf_op jit(solution)/shard_map/all_to_all | solution.py:72
  564.7 236.7 %all-to-all-start.3 = ((bf16[8,48,16384]{2,1,0:T(8,128)(2,1)}), bf16[8,48,16384]{2,1,0:T(8,128)(2,1)}, u32[]{:S(2)}, u32[]{:S(2)}) async-start(bf16[8,48,16384]{2,1,0:T(8,128)(2,1)} %fusion.22), calls=%async_computation.3 | async-start | bytes 25165824 | tf_op jit(solution)/shard_map/all_to_all | solution.py:14
  570.1 225.0 %all-reduce.3.cloned.1.call-start = ((), (), s32[]{:S(2)}) async-start(), calls=%async_computation.4 | async-start | bytes 5242880 | tf_op jit(solution)/shard_map/psum | solution.py:92
  614.6 106.2 %copy-start.8 = (f32[48,512]{1,0:T(8,128)S(1)}, f32[48,512]{1,0:T(8,128)}, u32[]{:S(2)}) copy-start(f32[48,512]{1,0:T(8,128)} %get-tuple-element.44) | copy-start | bytes 294916
  801.4 12.8 %copy-start.5 = (bf16[512,512]{1,0:T(8,128)(2,1)S(1)}, bf16[512,512]{1,0:T(8,128)(2,1)}, u32[]{:S(2)}) copy-start(bf16[512,512]{1,0:T(8,128)(2,1)} %param.15) | copy-start | bytes 1572868
  912.7 10.5 %copy-start.1 = (f32[384,512]{1,0:T(8,128)S(1)}, f32[384,512]{1,0:T(8,128)}, u32[]{:S(2)}) copy-start(f32[384,512]{1,0:T(8,128)} %param.16) | copy-start | bytes 2359300
Sparse Core Ops, SparseCore 0:
  614.7 180.2 all-reduce.2
